TPU v7x, 32 devices: a whole 2x2x4 slice. The times are simulated.
32 devices in a mesh: grid: 4 (over x, core), comp: 8 (over z, y).
Axes of the slice: x: 2, y: 2, z: 4, core: 2. Of those that a mesh axis runs over, the one named last changes fastest.
Arguments:
- spectra: float32 [32, 32, 36, 2048], P('comp', None, None, 'grid'), may hold values from 0.1 to 2
- u_wind: float32 [32, 2048], P(None, 'grid'), may hold values from 2 to 20
- wind_dir: float32 [32, 2048], P(None, 'grid'), may hold values from -3.140625 to 3.140625
- sea_mask: int32 [32, 2048], P(None, 'grid'), may hold values from 0 to 1, as said below
Outputs:
- spectra_next: float32 [32, 32, 36, 2048], P('comp', None, None, 'grid')
Inputs may be any that keep to these rules, and one draw needn't show every extreme that they name: sea_mask is 1 at sea and 0 on land; land lies in rectangular blocks of rows and columns.
All inputs are finite; a program needn't handle non-finite values.
Results may differ from a plain program's by a relative error of at most 0.00016.
Values sent between devices are 32-bit elements; how exact they have to be, the bound alone decides.
No kernel may reach another device: no remote copies, remote signals or barrier semaphores. Data moves between devices by JAX's collectives and lax.ppermute only.
A program may use at most 192 MiB of HBM per device.

v0:
```python
import math
import jax
import jax.numpy as jnp
from jax import lax
from jax.sharding import PartitionSpec as P

GRAVITY = 9.81
FREQ_LOW = 0.04
FREQ_RATIO = 1.1
LAMBDA = 0.25
SOURCE_STEP = 120.0
ADVECT_STEP = 220.0
WIND_FACTOR = 0.0003125
TRANSFER_FACTOR = 0.1
EARTH_RADIUS = 6371000.0
BAND_CENTRE = 30.0
CELL_DEGREES = 0.05
CELL_RADIANS = CELL_DEGREES * math.pi / 180.0
ANGLE_NEAR = 11.48
ANGLE_FAR = 33.56
FREQ_UPPER_SHIFT = math.log(1.0 + LAMBDA) / math.log(FREQ_RATIO)
FREQ_LOWER_SHIFT = math.log(1.0 - LAMBDA) / math.log(FREQ_RATIO)
WEIGHT_UPPER = 1.0 / (1.0 + LAMBDA) ** 4
WEIGHT_LOWER = 1.0 / (1.0 - LAMBDA) ** 4
WEIGHT_CROSS = 2.0 / (1.0 - LAMBDA * LAMBDA) ** 4
HIGHEST = lax.Precision.HIGHEST


def padded_2(block, sides, width):
    for axis, dim in sides:
        count = lax.axis_size(axis)
        forward = [(i, i + 1) for i in range(count - 1)]
        backward = [(target, source) for source, target in forward]
        low = lax.ppermute(
            lax.slice_in_dim(block, block.shape[dim] - width, None, axis=dim), axis, forward
        )
        high = lax.ppermute(lax.slice_in_dim(block, 0, width, axis=dim), axis, backward)
        block = jnp.concatenate([low, block, high], axis=dim)
    return block


def hat_matrix(bin_count, bin_shift, periodic):
    target = jnp.arange(bin_count, dtype=jnp.float32)[:, None] + bin_shift
    source = jnp.arange(bin_count, dtype=jnp.float32)[None, :]
    offset_gap = target - source
    if periodic:
        offset_gap = jnp.mod(offset_gap + bin_count / 2.0, float(bin_count)) - bin_count / 2.0
    return jnp.maximum(0.0, 1.0 - jnp.abs(offset_gap))


def nonlinear(point_block):
    freq_count = point_block.shape[0]
    dir_count = point_block.shape[2]
    freq_upper = hat_matrix(freq_count, FREQ_UPPER_SHIFT, False)
    freq_lower = hat_matrix(freq_count, FREQ_LOWER_SHIFT, False)
    spread_upper = jnp.einsum("km,mrjq->krjq", freq_upper, point_block, precision=HIGHEST)
    spread_lower = jnp.einsum("km,mrjq->krjq", freq_lower, point_block, precision=HIGHEST)
    near_bins = ANGLE_NEAR * dir_count / 360.0
    far_bins = ANGLE_FAR * dir_count / 360.0
    squared = point_block * point_block
    centre_total = jnp.zeros_like(point_block)
    back_upper = jnp.zeros_like(point_block)
    back_lower = jnp.zeros_like(point_block)
    for shifts in ((near_bins, -far_bins), (-near_bins, far_bins)):
        dir_upper = hat_matrix(dir_count, shifts[0], True)
        dir_lower = hat_matrix(dir_count, shifts[1], True)
        plus_value = jnp.einsum("jn,krnq->krjq", dir_upper, spread_upper, precision=HIGHEST)
        minus_value = jnp.einsum("jn,krnq->krjq", dir_lower, spread_lower, precision=HIGHEST)
        interaction = TRANSFER_FACTOR * (
            squared * (plus_value * WEIGHT_UPPER + minus_value * WEIGHT_LOWER)
            - WEIGHT_CROSS * point_block * plus_value * minus_value
        )
        centre_total = centre_total - 2.0 * interaction
        back_upper = back_upper + jnp.einsum(
            "jn,krjq->krnq", dir_upper, interaction, precision=HIGHEST
        )
        back_lower = back_lower + jnp.einsum(
            "jn,krjq->krnq", dir_lower, interaction, precision=HIGHEST
        )
    centre_total = centre_total + jnp.einsum(
        "km,krjq->mrjq", freq_upper, back_upper, precision=HIGHEST
    )
    return centre_total + jnp.einsum("km,krjq->mrjq", freq_lower, back_lower, precision=HIGHEST)


def frequency(freq_index):
    return (FREQ_LOW * jnp.power(FREQ_RATIO, freq_index.astype(jnp.float32))).reshape(-1, 1, 1, 1)


def wind_growth(freq, angles, wind_speed, heading):
    radian_freq = 2.0 * math.pi * freq
    celerity = GRAVITY / radian_freq
    alignment = jnp.cos(angles) * jnp.cos(heading) + jnp.sin(angles) * jnp.sin(heading)
    return (
        WIND_FACTOR
        * SOURCE_STEP
        * radian_freq
        * jnp.maximum(0.0, wind_speed / celerity * alignment - 1.0)
    )


def courant_x(freq, angles, row_index, total_rows):
    group_speed = GRAVITY / (4.0 * math.pi * freq)
    latitude = BAND_CENTRE + (row_index.astype(jnp.float32) - (total_rows - 1) / 2.0) * CELL_DEGREES
    row_cos = jnp.cos(latitude * (math.pi / 180.0)).reshape(1, -1, 1, 1)
    return group_speed * jnp.cos(angles) * ADVECT_STEP / (EARTH_RADIUS * row_cos * CELL_RADIANS)


def courant_y(freq, angles):
    group_speed = GRAVITY / (4.0 * math.pi * freq)
    return group_speed * jnp.sin(angles) * ADVECT_STEP / (EARTH_RADIUS * CELL_RADIANS)


def latitude_cos(total_rows):
    cell_lat = (
        BAND_CENTRE
        + (jnp.arange(total_rows, dtype=jnp.float32) - (total_rows - 1) / 2.0) * CELL_DEGREES
    )
    face_lat = (
        BAND_CENTRE
        + (jnp.arange(total_rows + 1, dtype=jnp.float32) - total_rows / 2.0) * CELL_DEGREES
    )
    cell_cos = jnp.cos(cell_lat * (math.pi / 180.0)).reshape(1, -1, 1, 1)
    face_cos = jnp.cos(face_lat * (math.pi / 180.0)).reshape(1, -1, 1, 1)
    return (face_cos, 1.0 / cell_cos)


def advect(padded, courant, face_weight, cell_weight, along_axis):
    cells = padded.shape[along_axis] - 4

    def piece_at(offset_cells, length_cells):
        return lax.slice_in_dim(padded, offset_cells, offset_cells + length_cells, axis=along_axis)

    left_cell = piece_at(1, cells + 1)
    right_cell = piece_at(2, cells + 1)
    far_left = piece_at(0, cells + 1)
    far_right = piece_at(3, cells + 1)
    curvature = jnp.where(
        courant >= 0.0,
        right_cell - 2.0 * left_cell + far_left,
        far_right - 2.0 * right_cell + left_cell,
    )
    face_value = (
        0.5 * (left_cell + right_cell)
        - 0.5 * courant * (right_cell - left_cell)
        - (1.0 - courant * courant) / 6.0 * curvature
    )
    flux_face = courant * face_value * face_weight
    difference = lax.slice_in_dim(flux_face, 1, cells + 1, axis=along_axis) - lax.slice_in_dim(
        flux_face, 0, cells, axis=along_axis
    )
    return piece_at(2, cells) - difference * cell_weight


def shards(spectra, u_wind, wind_dir, sea_mask):
    freq_local, band_rows, dir_count, lon_cells = spectra.shape
    comp_count = lax.axis_size("comp")
    block_rows = band_rows // comp_count
    comp_index = lax.axis_index("comp")
    mask_field = sea_mask.astype(jnp.float32)[None, :, None, :]
    masked = spectra * mask_field
    angles = (jnp.arange(dir_count, dtype=jnp.float32) * (2.0 * math.pi / dir_count)).reshape(
        1, 1, -1, 1
    )
    own_freq = frequency(comp_index * freq_local + jnp.arange(freq_local, dtype=jnp.int32))
    flattened = masked.reshape(freq_local, comp_count, block_rows, dir_count, lon_cells)
    point_block = lax.all_to_all(flattened, "comp", split_axis=1, concat_axis=0, tiled=True)[:, 0]
    all_freq = frequency(jnp.arange(freq_local * comp_count, dtype=jnp.int32))
    start_row = comp_index * block_rows
    speed_rows = lax.dynamic_slice_in_dim(u_wind, start_row, block_rows, 0)[None, :, None, :]
    heading_rows = lax.dynamic_slice_in_dim(wind_dir, start_row, block_rows, 0)[None, :, None, :]
    growth = wind_growth(all_freq, angles, speed_rows, heading_rows)
    post = point_block * (1.0 + growth) + nonlinear(point_block)
    padded = padded_2(post, (("grid", 3),), 2)
    mask_rows = lax.dynamic_slice_in_dim(sea_mask, start_row, block_rows, 0).astype(jnp.float32)[
        None, :, None, :
    ]
    row_index = start_row + jnp.arange(block_rows, dtype=jnp.int32)
    crossing = courant_x(all_freq, angles, row_index, band_rows)
    swept_points = advect(padded, crossing, 1.0, 1.0, 3) * mask_rows
    swept_x = lax.all_to_all(swept_points[:, None], "comp", split_axis=0, concat_axis=1, tiled=True)
    swept_x = swept_x.reshape(freq_local, band_rows, dir_count, lon_cells)
    padded_rows = jnp.pad(swept_x, ((0, 0), (2, 2), (0, 0), (0, 0)))
    face_cos, cell_inverse = latitude_cos(band_rows)
    return advect(padded_rows, courant_y(own_freq, angles), face_cos, cell_inverse, 1) * mask_field


def solution(mesh):
    return jax.shard_map(
        shards,
        mesh=mesh,
        in_specs=(P("comp", None, None, "grid"), P(None, "grid"), P(None, "grid"), P(None, "grid")),
        out_specs=P("comp", None, None, "grid"),
        check_vma=False,
    )
```

profile of v0, /device:TPU:1, one launch (start us, length us, event | category | flops | bytes accessed | tf_op | source)
XLA Modules:
  0.0 902.1 jit_solution(3873852487964017667)
XLA Ops:
  1.5 9.7 %broadcast_multiply_fusion.2 = f32[4,32,36,512]{3,1,2,0:T(8,128)} fusion(f32[4,32,36,512]{3,1,2,0:T(8,128)} %param.4, f32[32,512]{1,0:T(8,128)S(1)} %convert_element_type.37), kind=kLoop, calls=%fused_computation.70 | loop fusion | flops 2359296 | bytes 18939904 | tf_op jit(solution)/shard_map/mul | solution.py:161
  11.2 13.4 %copy.35 = f32[4,32,36,512]{3,0,2,1:T(4,128)} copy(f32[4,32,36,512]{3,1,2,0:T(8,128)} %broadcast_multiply_fusion.2) | data formatting | bytes 18874368 | tf_op jit(solution)/shard_map/mul | solution.py:161
  24.6 6.6 all-to-all-start
  34.0 201.9 %all-to-all-done = f32[4,8,4,36,512]{4,0,3,2,1:T(4,128)} async-done(((f32[4,8,4,36,512]{4,0,3,2,1:T(4,128)}), f32[4,8,4,36,512]{4,0,3,2,1:T(4,128)}, u32[]{:S(2)}, u32[]{:S(2)}) %all-to-all-start) | async-done | bytes 9437216 | tf_op jit(solution)/shard_map/all_to_all | solution.py:167
  235.9 10.3 %copy.36 = f32[8,4,1,4,36,512]{5,1,0,4,3,2:T(4,128)} copy(f32[8,4,1,4,36,512]{5,1,4,3,0,2:T(4,128)} %bitcast.2) | data formatting | bytes 18874368 | tf_op jit(solution)/shard_map/all_to_all | solution.py:167
  246.3 12.0 %squeeze.3 = f32[32,4,36,512]{3,0,2,1:T(8,128)} reshape(f32[8,4,1,4,36,512]{5,1,0,4,3,2:T(4,128)} %copy.36) | data formatting | bytes 18874368 | tf_op jit(solution)/shard_map/squeeze | solution.py:167
  258.2 13.3 %fusion.97 = f32[32,4,36,512]{3,0,2,1:T(8,128)S(1)} fusion(f32[32,4,36,512]{3,0,2,1:T(8,128)} %squeeze.3, f32[32]{0:T(128)S(1)} %get-tuple-element.19), kind=kOutput, calls=%fused_computation.122 | convolution fusion | flops 905973760 | bytes 18874496 | tf_op jit(solution)/shard_map/km,mrjq->krjq/dot_general | solution.py:56
  271.5 21.1 %fusion.27 = f32[32,4,512,36]{2,3,1,0:T(8,128)} fusion(f32[32,4,36,512]{3,0,2,1:T(8,128)S(1)} %fusion.97, f32[36]{0:T(128)S(1)} %iota_add_fusion.2), kind=kOutput, calls=%fused_computation.37 | convolution fusion | flops 1019231424 | bytes 18874512 | tf_op jit(solution)/shard_map/jn,krnq->krjq/dot_general | solution.py:67
  292.7 21.4 %fusion.29 = f32[32,4,512,36]{2,3,1,0:T(8,128)} fusion(f32[32,4,36,512]{3,0,2,1:T(8,128)S(1)} %fusion.97, f32[36]{0:T(128)S(1)} %iota_add_fusion.5), kind=kOutput, calls=%fused_computation.39 | convolution fusion | flops 1019231424 | bytes 18874512 | tf_op jit(solution)/shard_map/jn,krnq->krjq/dot_general | solution.py:67
  314.2 9.3 %fusion.94 = f32[32,4,36,512]{3,0,2,1:T(8,128)S(1)} fusion(f32[32,4,36,512]{3,0,2,1:T(8,128)S(1)} %bitcast.116, f32[32]{0:T(128)S(1)} %iota_add_fusion.4), kind=kOutput, calls=%fused_computation.119 | convolution fusion | flops 905973760 | bytes 18874496 | tf_op jit(solution)/shard_map/km,mrjq->krjq/dot_general | solution.py:57
  323.5 21.0 %fusion.23 = f32[32,4,512,36]{2,3,1,0:T(8,128)} fusion(f32[32,4,36,512]{3,0,2,1:T(8,128)S(1)} %fusion.94, f32[36]{0:T(128)S(1)} %iota_add_fusion.1), kind=kOutput, calls=%fused_computation.33 | convolution fusion | flops 1019231424 | bytes 18874512 | tf_op jit(solution)/shard_map/jn,krnq->krjq/dot_general | solution.py:68
  344.5 21.1 %fusion.25 = f32[32,4,512,36]{2,3,1,0:T(8,128)} fusion(f32[32,4,36,512]{3,0,2,1:T(8,128)S(1)} %fusion.94, f32[36]{0:T(128)S(1)} %iota_add_fusion.3), kind=kOutput, calls=%fused_computation.35 | convolution fusion | flops 1019231424 | bytes 18874512 | tf_op jit(solution)/shard_map/jn,krnq->krjq/dot_general | solution.py:68
  365.6 39.8 %broadcast_multiply_fusion.1 = (f32[32,4,36,512]{3,0,2,1:T(8,128)}, f32[32,4,36,512]{3,0,2,1:T(8,128)S(1)}) fusion(f32[32,4,36,512]{3,0,2,1:T(8,128)S(1)} %bitcast.116, f32[32,4,512,36]{2,3,1,0:T(8,128)} %fusion.25, f32[32,4,512,36]{2,3,1,0:T(8,128)} %fusion.29, f32[32,4,512,36]{2,3,1,0:T(8,128)} %fusion.23, f32[32,4,512,36]{2,3,1,0:T(8,128)} %fusion.27), kind=kLoop, calls=%fused_computation.69 | loop fusion | flops 42467328 | bytes 66060288 | tf_op jit(solution)/shard_map/mul | solution.py:69
  405.4 21.7 %fusion.15 = f32[32,4,512,36]{2,3,1,0:T(8,128)} fusion(f32[32,4,36,512]{3,0,2,1:T(8,128)S(1)} %get-tuple-element.8, f32[36]{0:T(128)S(1)} %iota_add_fusion.1), kind=kOutput, calls=%fused_computation.25 | convolution fusion | flops 1019231424 | bytes 18874512 | tf_op jit(solution)/shard_map/jn,krjq->krnq/dot_general | solution.py:77
  427.1 21.2 %fusion.17 = f32[32,4,512,36]{2,3,1,0:T(8,128)} fusion(f32[32,4,36,512]{3,0,2,1:T(8,128)S(1)} %get-tuple-element.8, f32[36]{0:T(128)S(1)} %iota_add_fusion.2), kind=kOutput, calls=%fused_computation.27 | convolution fusion | flops 1019231424 | bytes 18874512 | tf_op jit(solution)/shard_map/jn,krjq->krnq/dot_general | solution.py:74
  448.4 22.5 %add_bitcast_fusion = f32[32,4,36,512]{3,2,1,0:T(8,128)} fusion(f32[32,4,512,36]{2,3,1,0:T(8,128)} %fusion.15, f32[32,4,36,512]{3,0,2,1:T(8,128)S(1)} %bitcast.120, f32[36]{0:T(128)S(1)} %iota_add_fusion.3), kind=kOutput, calls=%fused_computation.23 | convolution fusion | flops 1021590720 | bytes 28311696 | tf_op jit(solution)/shard_map/jn,krjq->krnq/dot_general | solution.py:77
  470.9 19.4 %fusion.43 = f32[32,4,36,512]{3,0,2,1:T(8,128)} fusion(f32[32,4,36,512]{3,2,1,0:T(8,128)} %add_bitcast_fusion, f32[32]{0:T(128)S(1)} %iota_add_fusion.4), kind=kOutput, calls=%fused_computation.63 | convolution fusion | flops 905973760 | bytes 18874496 | tf_op jit(solution)/shard_map/km,krjq->mrjq/dot_general | solution.py:83
  490.4 23.0 %add_bitcast_fusion.1 = f32[32,4,36,512]{3,2,1,0:T(8,128)} fusion(f32[32,4,512,36]{2,3,1,0:T(8,128)S(1)} %bitcast.122, f32[32,4,36,512]{3,0,2,1:T(8,128)S(1)} %bitcast.120, f32[36]{0:T(128)S(1)} %iota_add_fusion.5), kind=kOutput, calls=%fused_computation.24 | convolution fusion | flops 1021590720 | bytes 28311696 | tf_op jit(solution)/shard_map/jn,krjq->krnq/dot_general | solution.py:74
  513.4 63.4 %add_add_fusion = f32[32,4,36,512]{3,0,2,1:T(8,128)} fusion(f32[32,4,36,512]{3,0,2,1:T(8,128)} %fusion.43, f32[32,4,36,512]{3,0,2,1:T(8,128)} %squeeze.3, f32[4,36,512]{2,1,0:T(8,128)S(1)} %multiply_add_fusion, f32[32,4,512]{2,0,1:T(8,128)S(1)} %broadcast_divide_fusion, f32[32]{0:T(128)S(1)} %get-tuple-element.20, ...), kind=kOutput, calls=%fused_computation.67 | convolution fusion | flops 974393344 | bytes 76054784 | tf_op jit(solution)/shard_map/km,krjq->mrjq/dot_general | solution.py:80
  576.9 4.7 fusion.211
  584.5 4.8 collective-permute-start
  594.0 3.0 copy.58
  598.0 4.3 copy.60
  602.3 22.3 %fusion.13 = f32[32,4,36,513]{3,0,2,1:T(8,128)S(1)} fusion(f32[32,4,36,2]{3,0,2,1:T(8,128)} %copy.60, f32[32,4,36,512]{3,0,2,1:T(8,128)} %add_add_fusion, f32[32,4,36,2]{3,0,2,1:T(8,128)S(1)} %copy.58, f32[32,4,36]{0,2,1:T(8,128)} %get-tuple-element.13, f32[32,4,36]{0,2,1:T(8,128)} %get-tuple-element.12, f32[32,4,36]{0,2,1:T(8,128)S(1)} %copy-done.5, ...), kind=kLoop, calls=%fused_computation.18 | loop fusion | flops 44914176 | bytes 19026432 | tf_op jit(solution)/shard_map/mul | solution.py:148
  624.7 5.4 fusion.36
  630.1 13.4 %copy.61 = f32[32,1,4,36,512]{4,2,3,1,0:T(4,128)} copy(f32[32,1,4,36,512]{4,0,3,2,1:T(8,128)} %fusion.36) | data formatting | bytes 18874368 | tf_op jit(solution)/shard_map/broadcast_in_dim | solution.py:181
  643.5 5.4 all-to-all-start.1
  649.2 203.8 %all-to-all-done.1 = f32[32,1,4,36,512]{4,2,3,1,0:T(4,128)} async-done(((f32[32,1,4,36,512]{4,2,3,1,0:T(4,128)}), f32[32,1,4,36,512]{4,2,3,1,0:T(4,128)}, u32[]{:S(2)}, u32[]{:S(2)}) %all-to-all-start.1) | async-done | bytes 9437216 | tf_op jit(solution)/shard_map/all_to_all | solution.py:181
  853.0 10.3 %copy.62 = f32[4,8,1,4,36,512]{5,3,1,4,0,2:T(4,128)} copy(f32[4,8,1,4,36,512]{5,3,4,0,1,2:T(4,128)} %bitcast.29) | data formatting | bytes 18874368 | tf_op jit(solution)/shard_map/all_to_all | solution.py:181
  863.3 11.9 %reshape.297 = f32[4,32,36,512]{3,1,2,0:T(8,128)} reshape(f32[4,8,1,4,36,512]{5,3,1,4,0,2:T(4,128)} %copy.62) | data formatting | bytes 18874368 | tf_op jit(solution)/shard_map/reshape | solution.py:182
  875.3 20.4 %fusion.5 = f32[4,33,36,512]{3,1,2,0:T(8,128)S(1)} fusion(f32[4,32,36,512]{3,1,2,0:T(8,128)} %reshape.297, f32[33]{0:T(128)S(1)} %multiply_cosine_fusion, f32[4,36]{1,0:T(4,128)S(1)} %get-tuple-element.16, f32[4,36]{1,0:T(4,128)S(1)} %get-tuple-element.15, f32[4,36]{1,0:T(4,128)S(1)} %get-tuple-element.14, pred[4,36]{1,0:T(4,128)(4,1)S(1)} %fusion.159), kind=kLoop, calls=%fused_computation.9 | loop fusion | flops 38928384 | bytes 19171284 | tf_op jit(solution)/shard_map/mul | solution.py:148
  895.7 5.9 fusion.33
  (75 shorter events, 13.2 us)
Async XLA Ops:
  0.0 31.4 %copy-start = (f32[32,512]{1,0:T(8,128)S(1)}, f32[32,512]{1,0:T(8,128)}, u32[]{:S(2)}) copy-start(f32[32,512]{1,0:T(8,128)} %param.5) | copy-start | bytes 196612
  0.9 0.6 copy-start.3
  24.6 211.4 %all-to-all-start = ((f32[4,8,4,36,512]{4,0,3,2,1:T(4,128)}), f32[4,8,4,36,512]{4,0,3,2,1:T(4,128)}, u32[]{:S(2)}, u32[]{:S(2)}) async-start(f32[4,8,4,36,512]{4,0,3,2,1:T(4,128)} %bitcast.123), calls=%async_computation | async-start | bytes 18874368 | tf_op jit(solution)/shard_map/all_to_all | solution.py:167
  31.4 2.5 copy-start.7
  271.5 42.6 %slice-start = ((s8[9437184]{0:T(1024)(128)(4,1)}), s8[4194304]{0:T(1024)(128)(4,1)S(1)}, s32[]{:S(2)}) async-start(s8[9437184]{0:T(1024)(128)(4,1)} %bitcast.115), calls=%async_computation.2 | async-start | bytes 8388608
  271.5 42.6 %slice-start.1 = ((s8[9437184]{0:T(1024)(128)(4,1)}), s8[4194304]{0:T(1024)(128)(4,1)S(1)}, s32[]{:S(2)}) async-start(s8[9437184]{0:T(1024)(128)(4,1)} %bitcast.115), calls=%async_computation.3 | async-start | bytes 8388608
  292.7 21.5 %slice-start.2 = ((s8[9437184]{0:T(1024)(128)(4,1)}), s8[1048576]{0:T(1024)(128)(4,1)S(1)}, s32[]{:S(2)}) async-start(s8[9437184]{0:T(1024)(128)(4,1)} %bitcast.115), calls=%async_computation.4 | async-start | bytes 2097152
  405.4 42.9 %slice-start.6 = ((s8[9437184]{0:T(1024)(128)(4,1)}), s8[4194304]{0:T(1024)(128)(4,1)S(1)}, s32[]{:S(2)}) async-start(s8[9437184]{0:T(1024)(128)(4,1)} %bitcast.119), calls=%async_computation.8 | async-start | bytes 8388608
  405.4 42.9 %slice-start.7 = ((s8[9437184]{0:T(1024)(128)(4,1)}), s8[4194304]{0:T(1024)(128)(4,1)S(1)}, s32[]{:S(2)}) async-start(s8[9437184]{0:T(1024)(128)(4,1)} %bitcast.119), calls=%async_computation.9 | async-start | bytes 8388608
  427.1 21.2 %slice-start.8 = ((s8[9437184]{0:T(1024)(128)(4,1)}), s8[1048576]{0:T(1024)(128)(4,1)S(1)}, s32[]{:S(2)}) async-start(s8[9437184]{0:T(1024)(128)(4,1)} %bitcast.119), calls=%async_computation.10 | async-start | bytes 2097152
  448.4 42.0 %slice-start.9 = ((s8[10485760]{0:T(1024)(128)(4,1)}), s8[4194304]{0:T(1024)(128)(4,1)S(1)}, s32[]{:S(2)}) async-start(s8[10485760]{0:T(1024)(128)(4,1)} %bitcast.121), calls=%async_computation.11 | async-start | bytes 8388608
  448.4 42.0 %slice-start.10 = ((s8[10485760]{0:T(1024)(128)(4,1)}), s8[4194304]{0:T(1024)(128)(4,1)S(1)}, s32[]{:S(2)}) async-start(s8[10485760]{0:T(1024)(128)(4,1)} %bitcast.121), calls=%async_computation.12 | async-start | bytes 8388608
  470.9 19.5 %slice-start.11 = ((s8[10485760]{0:T(1024)(128)(4,1)}), s8[2097152]{0:T(1024)(128)(4,1)S(1)}, s32[]{:S(2)}) async-start(s8[10485760]{0:T(1024)(128)(4,1)} %bitcast.121), calls=%async_computation.13 | async-start | bytes 4194304
  576.8 25.5 %copy-start.5 = (f32[32,4,36]{0,2,1:T(8,128)S(1)}, f32[32,4,36]{0,2,1:T(8,128)}, u32[]{:S(2)}) copy-start(f32[32,4,36]{0,2,1:T(8,128)} %get-tuple-element.11) | copy-start | bytes 55300
  576.8 25.5 %copy-start.6 = (pred[32,4,36]{0,2,1:T(8,128)(4,1)S(1)}, pred[32,4,36]{0,2,1:T(8,128)(4,1)}, u32[]{:S(2)}) copy-start(pred[32,4,36]{0,2,1:T(8,128)(4,1)} %broadcast_compare_fusion) | copy-start | bytes 13828
  584.5 9.5 %collective-permute-start = (f32[32,4,36,2]{2,0,3,1:T(8,128)S(1)}, f32[32,4,36,2]{2,0,3,1:T(8,128)}, u32[]{:S(2)}, u32[]{:S(2)}) collective-permute-start(f32[32,4,36,2]{2,0,3,1:T(8,128)S(1)} %copy.57), channel_id=1, source_target_pairs={{0,8},{8,16},{16,24},{1,9},{9,17},{17,25},{2,10},{10,18},{18,26},{... | collective-permute-start | bytes 110600 | tf_op jit(solution)/shard_map/ppermute | solution.py:34
  591.4 6.6 collective-permute-start.1
  598.0 26.7 %slice-start.3 = ((s8[9437184]{0:T(1024)(128)(4,1)}), s8[1048576]{0:T(1024)(128)(4,1)S(1)}, s32[]{:S(2)}) async-start(s8[9437184]{0:T(1024)(128)(4,1)} %bitcast.117), calls=%async_computation.5 | async-start | bytes 2097152
  602.3 22.4 %slice-start.4 = ((s8[9437184]{0:T(1024)(128)(4,1)}), s8[4194304]{0:T(1024)(128)(4,1)S(1)}, s32[]{:S(2)}) async-start(s8[9437184]{0:T(1024)(128)(4,1)} %bitcast.117), calls=%async_computation.6 | async-start | bytes 8388608
  602.3 22.4 %slice-start.5 = ((s8[9437184]{0:T(1024)(128)(4,1)}), s8[4194304]{0:T(1024)(128)(4,1)S(1)}, s32[]{:S(2)}) async-start(s8[9437184]{0:T(1024)(128)(4,1)} %bitcast.117), calls=%async_computation.7 | async-start | bytes 8388608
  643.5 5.6 copy-start.8
  643.5 209.5 %all-to-all-start.1 = ((f32[32,1,4,36,512]{4,2,3,1,0:T(4,128)}), f32[32,1,4,36,512]{4,2,3,1,0:T(4,128)}, u32[]{:S(2)}, u32[]{:S(2)}) async-start(f32[32,1,4,36,512]{4,2,3,1,0:T(4,128)} %copy.61), calls=%async_computation.1 | async-start | bytes 18874368 | tf_op jit(solution)/shard_map/all_to_all | solution.py:181
  875.3 20.4 %copy-start.2 = (f32[4,32,36,512]{3,1,2,0:T(8,128)S(1)}, f32[4,32,36,512]{3,1,2,0:T(8,128)}, u32[]{:S(2)}) copy-start(f32[4,32,36,512]{3,1,2,0:T(8,128)} %reshape.297) | copy-start | bytes 28311556
  875.3 20.5 %copy-start.4 = (f32[32,512]{1,0:T(8,128)S(1)}, f32[32,512]{1,0:T(8,128)}, u32[]{:S(2)}) copy-start(f32[32,512]{1,0:T(8,128)} %copy-done.3) | copy-start | bytes 196612
  895.7 5.9 copy-start.1
where the time goes:
time: 909 us; the launch traced here: 902 us
  waiting for transfers between devices  407 us (45%)
  matrix products  279 us (31%)
  other arithmetic  107 us (12%)
  local copies, waits for them, and re-layouts  90 us (10%)
  starting transfers between devices  18.7 us (2%)
    all_to_all x1, waiting for transfers between devices, shards(): lax.all_to_all(swept_points[:, None], 'comp', split_axis=0, concat_axis=1...  204 us
    all_to_all x1, waiting for transfers between devices, shards(): lax.all_to_all(flattened, 'comp', split_axis=1, concat_axis=0, tiled=True)  202 us
    dot_general x1, matrix products, nonlinear(): jnp.einsum('km,krjq->mrjq', freq_upper, back_upper, precision=HIGHEST)  63.4 us
    dot_general x2, matrix products, nonlinear(): jnp.einsum('jn,krjq->krnq', dir_lower, interaction, precision=HIGHEST)  44.2 us
    dot_general x2, matrix products, nonlinear(): jnp.einsum('jn,krjq->krnq', dir_upper, interaction, precision=HIGHEST)  44.2 us
    mul x2, other arithmetic, advect(): flux_face = courant * face_value * face_weight  42.8 us
    dot_general x2, matrix products, nonlinear(): jnp.einsum('jn,krnq->krjq', dir_upper, spread_upper, precision=HIGHEST)  42.6 us
    dot_general x2, matrix products, nonlinear(): jnp.einsum('jn,krnq->krjq', dir_lower, spread_lower, precision=HIGHEST)  42.1 us
  transfers between devices with their start and end apart: 4, of which 3 were waited for; matrix products, arithmetic and copies ran while one was open for 1% of the time, Pallas kernels for 0%

commit v1 on v0

--- a/solution.py
+++ b/solution.py
@@ -24,6 +24,22 @@
 WEIGHT_LOWER = 1.0 / (1.0 - LAMBDA) ** 4
 WEIGHT_CROSS = 2.0 / (1.0 - LAMBDA * LAMBDA) ** 4
 HIGHEST = lax.Precision.HIGHEST
+
+
+def exchange_in_pairs(array, axis, split, join):
+    ways, here = (lax.axis_size(axis), lax.axis_index(axis))
+    width = array.shape[split] // ways
+    dims = list(array.shape)
+    dims[split] = width
+    height = dims[join]
+    dims[join] = height * ways
+    full = jnp.zeros(dims, array.dtype)
+    for mask in range(ways):
+        part = lax.dynamic_slice_in_dim(array, (here ^ mask) * width, width, axis=split)
+        if mask:
+            part = lax.ppermute(part, axis, [(d, d ^ mask) for d in range(ways)])
+        full = lax.dynamic_update_slice_in_dim(full, part, (here ^ mask) * height, axis=join)
+    return full
 
 
 def padded_2(block, sides, width):
@@ -164,7 +180,7 @@
     )
     own_freq = frequency(comp_index * freq_local + jnp.arange(freq_local, dtype=jnp.int32))
     flattened = masked.reshape(freq_local, comp_count, block_rows, dir_count, lon_cells)
-    point_block = lax.all_to_all(flattened, "comp", split_axis=1, concat_axis=0, tiled=True)[:, 0]
+    point_block = exchange_in_pairs(flattened, "comp", 1, 0)[:, 0]
     all_freq = frequency(jnp.arange(freq_local * comp_count, dtype=jnp.int32))
     start_row = comp_index * block_rows
     speed_rows = lax.dynamic_slice_in_dim(u_wind, start_row, block_rows, 0)[None, :, None, :]

time: 909 us -> 850 us (0.935)
  waiting for transfers between devices: 407 us -> 325 us
  starting transfers between devices: 18.7 us -> 67.9 us
  matrix products: 279 us -> 241 us
  local copies, waits for them, and re-layouts: 90 us -> 108 us
    all_to_all x1 -> x0, waiting for transfers between devices: 202 us -> none  [shards(): lax.all_to_all(flattened, 'comp', split_axis=1, concat_axis=0, tiled=True)]
    ppermute x0 -> x7, waiting for transfers between devices: none -> 119 us  [exchange_in_pairs(): part = lax.ppermute(part, axis, [(d, d ^ mask) for d in range(ways)])]
    dot_general x1, matrix products: 63.4 us -> 19.6 us  [nonlinear(): jnp.einsum('km,krjq->mrjq', freq_upper, back_upper, precision=HIGHEST)]
    all_to_all x1, starting transfers between devices: 5.44 us -> 48.5 us  [shards(): lax.all_to_all(swept_points[:, None], 'comp', split_axis=0, concat_axis=1...]
    mul x1, other arithmetic: 39.8 us -> 0.55 us  [wind_growth(): WIND_FACTOR * SOURCE_STEP * radian_freq]
    dot_general x2, matrix products: 42.6 us -> 64.9 us  [nonlinear(): jnp.einsum('jn,krnq->krjq', dir_upper, spread_upper, precision=HIGHEST)]
    add x0 -> x1, other arithmetic: none -> 22 us  [shards(): post = point_block * (1.0 + growth) + nonlinear(point_block)]
    dynamic_slice x0 -> x8, local copies, waits for them, and re-layouts: none -> 18.1 us  [exchange_in_pairs(): lax.dynamic_slice_in_dim(array, (here ^ mask) * width, width, axis=split)]
  transfers between devices with their start and end apart: 4 -> 10, of which waited for: 3 -> 5; matrix products, arithmetic and copies ran while one was open for 1% -> 5% of each run, Pallas kernels for 0% -> 0%
where the time goes in v1:
time: 850 us; the launch traced here: 841 us
  waiting for transfers between devices  325 us (38%)
  matrix products  241 us (28%)
  local copies, waits for them, and re-layouts  108 us (13%)
  other arithmetic  98.2 us (12%)
  starting transfers between devices  67.9 us (8%)
    all_to_all x1, waiting for transfers between devices, shards(): lax.all_to_all(swept_points[:, None], 'comp', split_axis=0, concat_axis=1...  204 us
    ppermute x7, waiting for transfers between devices, exchange_in_pairs(): part = lax.ppermute(part, axis, [(d, d ^ mask) for d in range(ways)])  119 us
    dot_general x2, matrix products, nonlinear(): jnp.einsum('jn,krnq->krjq', dir_upper, spread_upper, precision=HIGHEST)  64.9 us
    all_to_all x1, starting transfers between devices, shards(): lax.all_to_all(swept_points[:, None], 'comp', split_axis=0, concat_axis=1...  48.5 us
    mul x2, other arithmetic, advect(): flux_face = courant * face_value * face_weight  46.9 us
    dot_general x2, matrix products, nonlinear(): jnp.einsum('jn,krnq->krjq', dir_lower, spread_lower, precision=HIGHEST)  41.8 us
    dot_general x2, matrix products, nonlinear(): jnp.einsum('jn,krjq->krnq', dir_upper, interaction, precision=HIGHEST)  32.8 us
    dot_general x2, matrix products, nonlinear(): jnp.einsum('jn,krjq->krnq', dir_lower, interaction, precision=HIGHEST)  26.4 us
  transfers between devices with their start and end apart: 10, of which 5 were waited for; matrix products, arithmetic and copies ran while one was open for 5% of the time, Pallas kernels for 0%

profile of v1, /device:TPU:1, one launch (start us, length us, event | category | flops | bytes accessed | tf_op | source)
XLA Modules:
  0.0 840.6 jit_solution(7124358905017122853)
XLA Ops:
  1.5 9.7 %broadcast_multiply_fusion = f32[4,32,36,512]{3,1,2,0:T(8,128)} fusion(f32[4,32,36,512]{3,1,2,0:T(8,128)} %param.4, f32[32,512]{1,0:T(8,128)S(1)} %convert_element_type.37), kind=kLoop, calls=%fused_computation.78 | loop fusion | flops 2359296 | bytes 18939904 | tf_op jit(solution)/shard_map/mul | solution.py:177
  11.2 13.4 %copy.36 = f32[4,32,36,512]{3,0,2,1:T(4,128)} copy(f32[4,32,36,512]{3,1,2,0:T(8,128)} %broadcast_multiply_fusion) | data formatting | bytes 18874368 | tf_op jit(solution)/shard_map/mul | solution.py:177
  24.6 6.4 constant_dynamic-slice_fusion.1
  51.1 5.3 squeeze.19
  63.0 3.4 collective-permute-start.5
  69.1 41.0 %collective-permute-done.1 = f32[4,1,4,36,512]{4,2,3,1,0:T(4,128)} collective-permute-done((f32[4,1,4,36,512]{4,2,3,1,0:T(4,128)}, f32[4,1,4,36,512]{4,2,3,1,0:T(4,128)}, u32[]{:S(2)}, u32[]{:S(2)}) %collective-permute-start.1) | collective-permute-done | bytes 1179680 | tf_op jit(solution)/shard_map/ppermute | solution.py:40
  112.9 21.5 %collective-permute-done.2 = f32[4,1,4,36,512]{4,2,3,1,0:T(4,128)} collective-permute-done((f32[4,1,4,36,512]{4,2,3,1,0:T(4,128)}, f32[4,1,4,36,512]{4,2,3,1,0:T(4,128)}, u32[]{:S(2)}, u32[]{:S(2)}) %collective-permute-start.2) | collective-permute-done | bytes 1179680 | tf_op jit(solution)/shard_map/ppermute | solution.py:40
  139.8 56.6 %collective-permute-done.4 = f32[4,1,4,36,512]{4,2,3,1,0:T(4,128)} collective-permute-done((f32[4,1,4,36,512]{4,2,3,1,0:T(4,128)}, f32[4,1,4,36,512]{4,2,3,1,0:T(4,128)}, u32[]{:S(2)}, u32[]{:S(2)}) %collective-permute-start.4) | collective-permute-done | bytes 1179680 | tf_op jit(solution)/shard_map/ppermute | solution.py:40
  202.1 17.7 %fusion.48 = f32[32,4,36,512]{3,0,2,1:T(8,128)S(1)} fusion(f32[32,4,36,512]{3,2,1,0:T(8,128)} %bitcast_dynamic-update-slice_fusion, f32[32]{0:T(128)S(1)} %iota_add_fusion.4), kind=kOutput, calls=%fused_computation.70 | convolution fusion | flops 905973760 | bytes 18874496 | tf_op jit(solution)/shard_map/km,mrjq->krjq/dot_general | solution.py:73
  219.8 18.1 %fusion.50 = f32[32,4,36,512]{3,0,2,1:T(8,128)} fusion(f32[32,4,36,512]{3,2,1,0:T(8,128)} %bitcast_dynamic-update-slice_fusion, f32[32]{0:T(128)S(1)} %copy-done.10), kind=kOutput, calls=%fused_computation.72 | convolution fusion | flops 905973760 | bytes 18874496 | tf_op jit(solution)/shard_map/km,mrjq->krjq/dot_general | solution.py:72
  237.9 21.0 %fusion.25 = f32[32,4,512,36]{2,3,1,0:T(8,128)} fusion(f32[32,4,36,512]{3,0,2,1:T(8,128)S(1)} %fusion.48, f32[36]{0:T(128)S(1)} %copy-done.17), kind=kOutput, calls=%fused_computation.46 | convolution fusion | flops 1019231424 | bytes 18874512 | tf_op jit(solution)/shard_map/jn,krnq->krjq/dot_general | solution.py:84
  258.9 30.7 %fusion.20 = f32[32,4,36,512]{3,2,1,0:T(8,128)} fusion(f32[32,4,512,36]{2,3,1,0:T(8,128)} %fusion.25, f32[32,4,36,512]{3,2,1,0:T(8,128)} %bitcast_dynamic-update-slice_fusion, f32[32,4,36,512]{3,0,2,1:T(8,128)} %fusion.50, f32[36]{0:T(128)} %iota_add_fusion.2), kind=kOutput, calls=%fused_computation.31 | convolution fusion | flops 1040465088 | bytes 37748880 | tf_op jit(solution)/shard_map/jn,krnq->krjq/dot_general | solution.py:83
  289.6 15.4 %fusion.35 = f32[32,4,512,36]{2,3,1,0:T(8,128)} fusion(f32[32,4,36,512]{3,2,1,0:T(8,128)} %fusion.20, f32[36]{0:T(128)} %iota_add_fusion.2), kind=kOutput, calls=%fused_computation.56 | convolution fusion | flops 1021590720 | bytes 18874512 | tf_op jit(solution)/shard_map/jn,krjq->krnq/dot_general | solution.py:90
  305.0 12.4 %fusion.33 = f32[32,4,512,36]{2,3,1,0:T(8,128)} fusion(f32[32,4,36,512]{3,2,1,0:T(8,128)S(1)} %copy-done.2, f32[36]{0:T(128)S(1)} %copy-done.18), kind=kOutput, calls=%fused_computation.54 | convolution fusion | flops 1021590720 | bytes 18874512 | tf_op jit(solution)/shard_map/jn,krjq->krnq/dot_general | solution.py:93
  317.5 20.8 %fusion.27 = f32[32,4,512,36]{2,3,1,0:T(8,128)} fusion(f32[32,4,36,512]{3,0,2,1:T(8,128)S(1)} %fusion.48, f32[36]{0:T(128)S(1)} %copy-done.14), kind=kOutput, calls=%fused_computation.48 | convolution fusion | flops 1019231424 | bytes 18874512 | tf_op jit(solution)/shard_map/jn,krnq->krjq/dot_general | solution.py:84
  338.3 34.2 %fusion.23 = f32[32,4,36,512]{3,2,1,0:T(8,128)} fusion(f32[32,4,512,36]{2,3,1,0:T(8,128)} %fusion.27, f32[32,4,36,512]{3,2,1,0:T(8,128)} %bitcast_dynamic-update-slice_fusion, f32[32,4,36,512]{3,0,2,1:T(8,128)} %fusion.50, f32[36]{0:T(128)} %iota_add_fusion.5), kind=kOutput, calls=%fused_computation.38 | convolution fusion | flops 1040465088 | bytes 37748880 | tf_op jit(solution)/shard_map/jn,krnq->krjq/dot_general | solution.py:83
  372.6 17.4 %add_bitcast_fusion.1 = f32[32,4,36,512]{3,2,1,0:T(8,128)} fusion(f32[32,4,512,36]{2,3,1,0:T(8,128)} %fusion.35, f32[32,4,36,512]{3,2,1,0:T(8,128)} %fusion.23, f32[36]{0:T(128)S(1)} %copy-done.16), kind=kOutput, calls=%fused_computation.45 | convolution fusion | flops 1023950016 | bytes 28311696 | tf_op jit(solution)/shard_map/jn,krjq->krnq/dot_general | solution.py:90
  389.9 19.6 %fusion.46 = f32[32,4,36,512]{3,0,2,1:T(8,128)} fusion(f32[32,4,36,512]{3,2,1,0:T(8,128)} %add_bitcast_fusion.1, f32[32]{0:T(128)S(1)} %copy-done.11), kind=kOutput, calls=%fused_computation.68 | convolution fusion | flops 905973760 | bytes 18874496 | tf_op jit(solution)/shard_map/km,krjq->mrjq/dot_general | solution.py:96
  409.6 13.9 %add_bitcast_fusion = f32[32,4,36,512]{3,2,1,0:T(8,128)} fusion(f32[32,4,512,36]{2,3,1,0:T(8,128)} %fusion.33, f32[32,4,36,512]{3,2,1,0:T(8,128)S(1)} %bitcast.111, f32[36]{0:T(128)S(1)} %copy-done.15), kind=kOutput, calls=%fused_computation.44 | convolution fusion | flops 1023950016 | bytes 28311696 | tf_op jit(solution)/shard_map/jn,krjq->krnq/dot_general | solution.py:93
  423.5 19.6 %fusion.44 = f32[32,4,36,512]{3,0,2,1:T(8,128)} fusion(f32[32,4,36,512]{3,2,1,0:T(8,128)} %add_bitcast_fusion, f32[32]{0:T(128)S(1)} %iota_add_fusion.4), kind=kOutput, calls=%fused_computation.66 | convolution fusion | flops 905973760 | bytes 18874496 | tf_op jit(solution)/shard_map/km,krjq->mrjq/dot_general | solution.py:99
  443.2 22.0 %fusion.24 = f32[32,4,36,512]{3,2,1,0:T(8,128)} fusion(f32[32,4,36,512]{3,0,2,1:T(8,128)} %fusion.44, f32[32,4,36,512]{3,0,2,1:T(8,128)} %fusion.46, f32[32,4,36,512]{3,2,1,0:T(8,128)S(1)} %bitcast.109, f32[32,4,36,512]{3,2,1,0:T(8,128)S(1)} %bitcast.111, f32[32,4,36,512]{3,2,1,0:T(8,128)} %bitcast_dynamic-update-slice_fusion, ...), kind=kLoop, calls=%fused_computation.42 | loop fusion | flops 30670848 | bytes 57180288 | tf_op jit(solution)/shard_map/add | solution.py:189
  465.2 4.9 fusion.224
  472.8 7.2 collective-permute-start.7
  489.9 26.6 %fusion.5 = f32[32,4,36,513]{3,2,1,0:T(8,128)S(1)} fusion(f32[32,4,36,2]{3,2,1,0:T(8,128)} %copy.71, f32[32,4,36,512]{3,2,1,0:T(8,128)} %fusion.24, f32[32,4,36,2]{3,2,1,0:T(8,128)} %copy.69, f32[32,4,36]{2,1,0:T(4,128)S(1)} %copy-done.8, f32[32,4,36]{2,1,0:T(4,128)S(1)} %get-tuple-element.18, f32[32,4,36]{2,1,0:T(4,128)S(1)} %get-tuple-element.17, ...), kind=kLoop, calls=%fused_computation.10 | loop fusion | flops 44914176 | bytes 19026432 | tf_op jit(solution)/shard_map/mul | solution.py:164
  516.6 6.1 fusion.17
  522.7 15.7 %copy.72 = f32[32,1,4,36,512]{4,2,3,1,0:T(4,128)} copy(f32[32,1,4,36,512]{4,3,2,0,1:T(8,128)} %fusion.17) | data formatting | bytes 18874368 | tf_op jit(solution)/shard_map/broadcast_in_dim | solution.py:197
  538.4 48.5 %all-to-all-start = ((f32[32,1,4,36,512]{4,2,3,1,0:T(4,128)}), f32[32,1,4,36,512]{4,2,3,1,0:T(4,128)}, u32[]{:S(2)}, u32[]{:S(2)}) async-start(f32[32,1,4,36,512]{4,2,3,1,0:T(4,128)} %copy.72), calls=%async_computation | async-start | bytes 18874368 | tf_op jit(solution)/shard_map/all_to_all | solution.py:197
  587.2 204.5 %all-to-all-done = f32[32,1,4,36,512]{4,2,3,1,0:T(4,128)} async-done(((f32[32,1,4,36,512]{4,2,3,1,0:T(4,128)}), f32[32,1,4,36,512]{4,2,3,1,0:T(4,128)}, u32[]{:S(2)}, u32[]{:S(2)}) %all-to-all-start) | async-done | bytes 9437216 | tf_op jit(solution)/shard_map/all_to_all | solution.py:197
  791.7 10.3 %copy.73 = f32[4,8,1,4,36,512]{5,3,1,4,0,2:T(4,128)} copy(f32[4,8,1,4,36,512]{5,3,4,0,1,2:T(4,128)} %bitcast.35) | data formatting | bytes 18874368 | tf_op jit(solution)/shard_map/all_to_all | solution.py:197
  802.0 11.9 %reshape.312 = f32[4,32,36,512]{3,1,2,0:T(8,128)} reshape(f32[4,8,1,4,36,512]{5,3,1,4,0,2:T(4,128)} %copy.73) | data formatting | bytes 18874368 | tf_op jit(solution)/shard_map/reshape | solution.py:198
  813.9 20.3 %fusion.12 = f32[4,33,36,512]{3,1,2,0:T(8,128)S(1)} fusion(f32[4,32,36,512]{3,1,2,0:T(8,128)} %reshape.312, f32[33]{0:T(128)S(1)} %multiply_cosine_fusion, f32[4,36]{1,0:T(4,128)S(1)} %get-tuple-element.22, f32[4,36]{1,0:T(4,128)S(1)} %get-tuple-element.21, f32[4,36]{1,0:T(4,128)S(1)} %get-tuple-element.20, pred[4,36]{1,0:T(4,128)(4,1)S(1)} %fusion.168), kind=kLoop, calls=%fused_computation.20 | loop fusion | flops 38928384 | bytes 19171284 | tf_op jit(solution)/shard_map/mul | solution.py:164
  834.3 5.9 fusion.43
  (118 shorter events, 57.6 us)
Async XLA Ops:
  0.0 50.2 %copy-start = (f32[32,512]{1,0:T(8,128)S(1)}, f32[32,512]{1,0:T(8,128)}, u32[]{:S(2)}) copy-start(f32[32,512]{1,0:T(8,128)} %param.5) | copy-start | bytes 196612
  32.8 30.2 %collective-permute-start = (f32[4,1,4,36,512]{4,2,3,1,0:T(4,128)}, f32[4,1,4,36,512]{4,2,3,1,0:T(4,128)}, u32[]{:S(2)}, u32[]{:S(2)}) collective-permute-start(f32[4,1,4,36,512]{4,2,3,1,0:T(4,128)} %copy.38), channel_id=1, source_target_pairs={{0,1},{1,0},{2,3},{3,2},{4,5},{5,4},{6,7},{7,6},{8,9},{9,8},{10,11... | collective-permute-start | bytes 3538952 | tf_op jit(solution)/shard_map/ppermute | solution.py:40
  36.6 73.5 %collective-permute-start.1 = (f32[4,1,4,36,512]{4,2,3,1,0:T(4,128)}, f32[4,1,4,36,512]{4,2,3,1,0:T(4,128)}, u32[]{:S(2)}, u32[]{:S(2)}) collective-permute-start(f32[4,1,4,36,512]{4,2,3,1,0:T(4,128)} %copy.40), channel_id=1, source_target_pairs={{0,2},{1,3},{2,0},{3,1},{4,6},{5,7},{6,4},{7,5},{8,10},{9,11},{10,... | collective-permute-start | bytes 3538952 | tf_op jit(solution)/shard_map/ppermute | solution.py:40
  39.9 94.5 %collective-permute-start.2 = (f32[4,1,4,36,512]{4,2,3,1,0:T(4,128)}, f32[4,1,4,36,512]{4,2,3,1,0:T(4,128)}, u32[]{:S(2)}, u32[]{:S(2)}) collective-permute-start(f32[4,1,4,36,512]{4,2,3,1,0:T(4,128)} %copy.42), channel_id=1, source_target_pairs={{0,3},{1,2},{2,1},{3,0},{4,7},{5,6},{6,5},{7,4},{8,11},{9,10},{10,... | collective-permute-start | bytes 3538952 | tf_op jit(solution)/shard_map/ppermute | solution.py:40
  41.7 95.4 %collective-permute-start.3 = (f32[4,1,4,36,512]{4,2,3,1,0:T(4,128)}, f32[4,1,4,36,512]{4,2,3,1,0:T(4,128)}, u32[]{:S(2)}, u32[]{:S(2)}) collective-permute-start(f32[4,1,4,36,512]{4,2,3,1,0:T(4,128)} %copy.44), channel_id=1, source_target_pairs={{0,4},{1,5},{2,6},{3,7},{4,0},{5,1},{6,2},{7,3},{8,12},{9,13},{10,... | collective-permute-start | bytes 3538952 | tf_op jit(solution)/shard_map/ppermute | solution.py:40
  45.9 150.6 %collective-permute-start.4 = (f32[4,1,4,36,512]{4,2,3,1,0:T(4,128)}, f32[4,1,4,36,512]{4,2,3,1,0:T(4,128)}, u32[]{:S(2)}, u32[]{:S(2)}) collective-permute-start(f32[4,1,4,36,512]{4,2,3,1,0:T(4,128)} %copy.46), channel_id=1, source_target_pairs={{0,5},{1,4},{2,7},{3,6},{4,1},{5,0},{6,3},{7,2},{8,13},{9,12},{10,... | collective-permute-start | bytes 3538952 | tf_op jit(solution)/shard_map/ppermute | solution.py:40
  49.2 20.0 %copy-start.12 = (f32[36]{0:T(128)}, f32[36]{0:T(128)S(1)}, u32[]{:S(2)}) copy-start(f32[36]{0:T(128)S(1)} %get-tuple-element.23) | copy-start | bytes 436
  63.0 136.2 %collective-permute-start.5 = (f32[4,1,4,36,512]{4,2,3,1,0:T(4,128)}, f32[4,1,4,36,512]{4,2,3,1,0:T(4,128)S(1)}, u32[]{:S(2)}, u32[]{:S(2)}) collective-permute-start(f32[4,1,4,36,512]{4,2,3,1,0:T(4,128)} %copy.48), channel_id=1, source_target_pairs={{0,6},{1,7},{2,4},{3,5},{4,2},{5,3},{6,0},{7,1},{8,14},{9,15},{10,... | collective-permute-start | bytes 3538952 | tf_op jit(solution)/shard_map/ppermute | solution.py:40
  110.1 90.5 %collective-permute-start.6 = (f32[4,1,4,36,512]{4,2,3,1,0:T(4,128)S(1)}, f32[4,1,4,36,512]{4,2,3,1,0:T(4,128)S(1)}, u32[]{:S(2)}, u32[]{:S(2)}) collective-permute-start(f32[4,1,4,36,512]{4,2,3,1,0:T(4,128)S(1)} %copy.50), channel_id=1, source_target_pairs={{0,7},{1,6},{2,5},{3,4},{4,3},{5,2},{6,1},{7,0},{8,15},{9,14},{10,... | collective-permute-start | bytes 3538952 | tf_op jit(solution)/shard_map/ppermute | solution.py:40
  200.6 19.2 %copy-start.10 = (f32[32]{0:T(128)S(1)}, f32[32]{0:T(128)}, u32[]{:S(2)}) copy-start(f32[32]{0:T(128)} %iota_add_fusion.6) | copy-start | bytes 388
  338.3 34.2 %copy-start.16 = (f32[36]{0:T(128)S(1)}, f32[36]{0:T(128)}, u32[]{:S(2)}) copy-start(f32[36]{0:T(128)} %iota_add_fusion.5) | copy-start | bytes 436
  372.6 37.0 %slice-start.3 = ((s8[10485760]{0:T(1024)(128)(4,1)}), s8[4194304]{0:T(1024)(128)(4,1)S(1)}, s32[]{:S(2)}) async-start(s8[10485760]{0:T(1024)(128)(4,1)} %bitcast.110), calls=%async_computation.4 | async-start | bytes 8388608
  372.6 37.0 %slice-start.4 = ((s8[10485760]{0:T(1024)(128)(4,1)}), s8[4194304]{0:T(1024)(128)(4,1)S(1)}, s32[]{:S(2)}) async-start(s8[10485760]{0:T(1024)(128)(4,1)} %bitcast.110), calls=%async_computation.5 | async-start | bytes 8388608
  389.9 19.6 %slice-start.5 = ((s8[10485760]{0:T(1024)(128)(4,1)}), s8[2097152]{0:T(1024)(128)(4,1)S(1)}, s32[]{:S(2)}) async-start(s8[10485760]{0:T(1024)(128)(4,1)} %bitcast.110), calls=%async_computation.6 | async-start | bytes 4194304
  389.9 19.6 %copy-start.15 = (f32[36]{0:T(128)S(1)}, f32[36]{0:T(128)}, u32[]{:S(2)}) copy-start(f32[36]{0:T(128)} %iota_add_fusion.3) | copy-start | bytes 436
  409.5 33.6 %slice-start = ((s8[10485760]{0:T(1024)(128)(4,1)}), s8[4194304]{0:T(1024)(128)(4,1)S(1)}, s32[]{:S(2)}) async-start(s8[10485760]{0:T(1024)(128)(4,1)} %bitcast.108), calls=%async_computation.1 | async-start | bytes 8388608
  409.5 33.6 %slice-start.1 = ((s8[10485760]{0:T(1024)(128)(4,1)}), s8[2097152]{0:T(1024)(128)(4,1)S(1)}, s32[]{:S(2)}) async-start(s8[10485760]{0:T(1024)(128)(4,1)} %bitcast.108), calls=%async_computation.2 | async-start | bytes 4194304
  423.5 19.6 %slice-start.2 = ((s8[10485760]{0:T(1024)(128)(4,1)}), s8[4194304]{0:T(1024)(128)(4,1)S(1)}, s32[]{:S(2)}) async-start(s8[10485760]{0:T(1024)(128)(4,1)} %bitcast.108), calls=%async_computation.3 | async-start | bytes 8388608
  423.5 19.6 %copy-start.5 = (f32[32,4,512]{2,1,0:T(4,128)S(1)}, f32[32,4,512]{2,1,0:T(4,128)}, u32[]{:S(2)}) copy-start(f32[32,4,512]{2,1,0:T(4,128)} %broadcast_divide_fusion) | copy-start | bytes 786436
  423.5 19.6 %copy-start.19 = (f32[32]{0:T(128)S(1)}, f32[32]{0:T(128)}, u32[]{:S(2)}) copy-start(f32[32]{0:T(128)} %fusion.171) | copy-start | bytes 388
  465.2 24.7 %copy-start.8 = (f32[32,4,36]{2,1,0:T(4,128)S(1)}, f32[32,4,36]{2,1,0:T(4,128)}, u32[]{:S(2)}) copy-start(f32[32,4,36]{2,1,0:T(4,128)} %get-tuple-element.19) | copy-start | bytes 55300
  465.2 24.7 %copy-start.9 = (pred[32,4,36]{2,1,0:T(4,128)(4,1)S(1)}, pred[32,4,36]{2,1,0:T(4,128)(4,1)}, u32[]{:S(2)}) copy-start(pred[32,4,36]{2,1,0:T(4,128)(4,1)} %broadcast_compare_fusion) | copy-start | bytes 13828
  472.8 10.9 %collective-permute-start.7 = (f32[32,4,36,2]{2,0,3,1:T(8,128)S(1)}, f32[32,4,36,2]{2,0,3,1:T(8,128)S(1)}, u32[]{:S(2)}, u32[]{:S(2)}) collective-permute-start(f32[32,4,36,2]{2,0,3,1:T(8,128)S(1)} %copy.68), channel_id=1, source_target_pairs={{0,8},{8,16},{16,24},{1,9},{9,17},{17,25},{2,10},{10,18},{18,26},{... | collective-permute-start | bytes 110600 | tf_op jit(solution)/shard_map/ppermute | solution.py:50
  481.1 6.3 collective-permute-start.8
  487.4 29.2 %slice-start.6 = ((s8[10485760]{0:T(1024)(128)(4,1)}), s8[2097152]{0:T(1024)(128)(4,1)S(1)}, s32[]{:S(2)}) async-start(s8[10485760]{0:T(1024)(128)(4,1)} %bitcast.112), calls=%async_computation.7 | async-start | bytes 4194304
  489.9 26.7 %slice-start.7 = ((s8[10485760]{0:T(1024)(128)(4,1)}), s8[4194304]{0:T(1024)(128)(4,1)S(1)}, s32[]{:S(2)}) async-start(s8[10485760]{0:T(1024)(128)(4,1)} %bitcast.112), calls=%async_computation.8 | async-start | bytes 8388608
  489.9 26.7 %slice-start.8 = ((s8[10485760]{0:T(1024)(128)(4,1)}), s8[4194304]{0:T(1024)(128)(4,1)S(1)}, s32[]{:S(2)}) async-start(s8[10485760]{0:T(1024)(128)(4,1)} %bitcast.112), calls=%async_computation.9 | async-start | bytes 8388608
  538.4 48.7 %copy-start.13 = (f32[36]{0:T(128)S(1)}, f32[36]{0:T(128)}, u32[]{:S(2)}) copy-start(f32[36]{0:T(128)} %copy-done.12) | copy-start | bytes 436
  538.4 253.3 %all-to-all-start = ((f32[32,1,4,36,512]{4,2,3,1,0:T(4,128)}), f32[32,1,4,36,512]{4,2,3,1,0:T(4,128)}, u32[]{:S(2)}, u32[]{:S(2)}) async-start(f32[32,1,4,36,512]{4,2,3,1,0:T(4,128)} %copy.72), calls=%async_computation | async-start | bytes 18874368 | tf_op jit(solution)/shard_map/all_to_all | solution.py:197
  813.9 20.3 %copy-start.3 = (f32[4,32,36,512]{3,1,2,0:T(8,128)S(1)}, f32[4,32,36,512]{3,1,2,0:T(8,128)}, u32[]{:S(2)}) copy-start(f32[4,32,36,512]{3,1,2,0:T(8,128)} %reshape.312) | copy-start | bytes 28311556
  813.9 20.3 %copy-start.7 = (f32[32,512]{1,0:T(8,128)S(1)}, f32[32,512]{1,0:T(8,128)}, u32[]{:S(2)}) copy-start(f32[32,512]{1,0:T(8,128)} %copy-done.6) | copy-start | bytes 196612
  813.9 26.2 %copy-start.1 = (f32[32,512]{1,0:T(8,128)S(1)}, f32[32,512]{1,0:T(8,128)}, u32[]{:S(2)}) copy-start(f32[32,512]{1,0:T(8,128)} %param.5) | copy-start | bytes 196612
  (7 other events, 86.6 us)
